TPU v7x, 128 devices: a whole 4x4x4 slice. The times are simulated.
128 devices in a mesh: section: 8 (over y, core), row: 16 (over x, z).
Axes of the slice: x: 4, y: 4, z: 4, core: 2. Of those that a mesh axis runs over, the one named last changes fastest.
Arguments:
- coupling: bfloat16 [2048, 128, 128], P(('section', 'row')), may hold values from -4 to 4
- diag_inverse: float32 [2048, 128, 128], P(('section', 'row')), may hold values from -0.046875 to 0.046875
- pivot_inverse: bfloat16 [512, 128, 128], P(('section', 'row')), may hold values from -0.5 to 0.5
- cross_left: bfloat16 [16384, 128, 128], P(('section', 'row')), may hold values from -0.5 to 0.5
- cross_right: bfloat16 [16384, 128, 128], P(('section', 'row')), may hold values from -4 to 4
- cross_pivot: int32 [16384], P(('section', 'row')), may hold values from 0 to 3
- cross_owner: int32 [16384, 1], P(('section', 'row')), may hold values from 0 to 15; in each aligned block of 128 rows (0 to 127, 128 to 255, ...) at most 16 rows name the same one
- foreign_target_row: int32 [16384], P(('section', 'row')), may hold values from 0 to 15
- cross_count: int32 [128], P(('section', 'row')), may hold values from 1 to 128, 12288 in all
- local_left: bfloat16 [16384, 128, 128], P(('section', 'row')), may hold values from -0.5 to 0.5
- local_right: bfloat16 [16384, 128, 128], P(('section', 'row')), may hold values from -4 to 4
- local_pivot: int32 [16384], P(('section', 'row')), may hold values from 0 to 3
- local_target: int32 [16384], P(('section', 'row')), may hold values from 0 to 15
- adjoint_seed: float32 [2048, 128, 128], P(('section', 'row')), may hold values from -48 to 48
Outputs:
- coupling_new: float32 [2048, 128, 128], P(('section', 'row'))
- adjoint: float32 [2048, 128, 128], P(('section', 'row'))
Inputs may be any that keep to these rules, and one draw needn't show every extreme that they name: `cross_owner`: among the 128 cross slots of one device, live or not, at most 16 name the same owner, a bound that some block reaches of them. `cross_count`: some device has all its cross slots live.
All inputs are finite; a program needn't handle non-finite values.
Results may differ from a plain program's by a relative error of at most 0.0089.
Values may be sent and summed in bfloat16 or wider, within the bound.
No kernel may reach another device: no remote copies, remote signals or barrier semaphores. Data moves between devices by JAX's collectives and lax.ppermute only.
A program may use at most 192 MiB of HBM per device.

v0:
```python
import functools

import jax
import jax.numpy as jnp
from jax import lax
from jax.experimental import pallas as pl
from jax.experimental.pallas import tpu as pltpu
from jax.sharding import PartitionSpec as P

B = 128
SIDE = 4
UNROLL = 16
CHUNKS = 8
SIDE_BIT = 2
PLACES = sum(p << (3 * i) for i, p in enumerate((6, 7, 4, 2, 0, 1, 3, 5)))
CELL_MASK, PIVOT_BIT, FAR_BIT, NEAR_BIT, SLOT_BIT = 511, 9, 16, 17, 20
ORDER = (0, 2, 1, 3)
MIB = 1 << 20

ANY = pl.BlockSpec(memory_space=pl.ANY)
HBM = pl.BlockSpec(memory_space=pltpu.HBM)
VMEM = pl.BlockSpec(memory_space=pltpu.VMEM)
SMEM = pl.BlockSpec(memory_space=pltpu.SMEM)

bf16 = jnp.bfloat16
f32 = jnp.float32


def mm(a, b):
    return jnp.dot(a, b, preferred_element_type=f32)


def mm_nt(a, b):
    return lax.dot_general(a, b, (((1,), (1,)), ((), ())), preferred_element_type=f32)


def split(x):
    high = x.astype(bf16)
    return high, (x - high.astype(f32)).astype(bf16)


def stay(x):
    return pltpu.with_memory_space_constraint(x, pltpu.HBM)


def bulk(left_ref, right_ref, left, right, lsem, rsem):
    per = left.shape[0] // CHUNKS
    pairs = []
    for k in range(CHUNKS):
        part = pl.ds(k * per, per)
        pair = (
            pltpu.make_async_copy(left_ref.at[part], left.at[part], lsem.at[k]),
            pltpu.make_async_copy(right_ref.at[part], right.at[part], rsem.at[k]),
        )
        for c in pair:
            c.start()
        pairs.append(pair)
    return pairs


def sum_cells(first, flag, index_ref, listed, total, outs, ready, left, right, table):
    slots = left.shape[0]
    cells = total.shape[0] - 1

    def note(i, n):
        word = index_ref[i]
        listed[n] = word
        return n + ((word >> flag) & 1)

    count = lax.fori_loop(0, slots, note, 0, unroll=32)
    for u in range(UNROLL):
        listed[count + u] = first + cells

    def clear(c, _):
        total[c] = jnp.zeros((B, B), bf16)
        return 0

    lax.fori_loop(0, cells + 1, clear, 0, unroll=8)
    ready()

    def work(r, _):
        words = [listed[r * UNROLL + u] for u in range(UNROLL)]
        scaled = [mm(left[w >> SLOT_BIT], table[(w >> PIVOT_BIT) & 3]).astype(bf16) for w in words]
        updates = [mm(x, right[w >> SLOT_BIT]) for x, w in zip(scaled, words)]
        for w, u in zip(words, updates):
            c = (w & CELL_MASK) - first
            total[c] = (total[c].astype(f32) + u).astype(bf16)
        return 0

    lax.fori_loop(0, (count + UNROLL - 1) // UNROLL, work, 0)
    start = 0
    for out in outs:

        def give(c, _, out=out, start=start):
            out[c] = total[start + c]
            return 0

        lax.fori_loop(0, out.shape[0], give, 0, unroll=8)
        start += out.shape[0]


def far_kernel(half, owner_ref, target_ref, pivot_ref, count_ref, table_ref, left_ref, right_ref, *refs):
    *outs, left, right, table, index_ref, owner, target, pivot, index, listed, total, lsem, rsem, tsem, isem = refs
    slots = left.shape[0]
    given = [
        pltpu.make_async_copy(x, y, isem.at[k])
        for k, (x, y) in enumerate(((owner_ref, owner), (target_ref, target), (pivot_ref, pivot)))
    ]
    for c in given:
        c.start()
    pairs = bulk(left_ref, right_ref, left, right, lsem, rsem)
    table_copy = pltpu.make_async_copy(table_ref, table, tsem)
    table_copy.start()
    for c in given:
        c.wait()

    odd = lax.axis_index("section") % 2
    me = lax.axis_index("row")
    first_shift = jnp.where(odd == 0, SIDE_BIT, 0)
    second_shift = SIDE_BIT - first_shift
    first_me, second_me = me >> first_shift, me >> second_shift
    live = count_ref[0]
    half_bit = half.bit_length() - 1
    per_bit = half_bit + SIDE_BIT

    def word(i, _):
        a = ((owner[i] >> first_shift) - first_me) & (SIDE - 1)
        b = ((owner[i] >> second_shift) - second_me) & (SIDE - 1)
        place = (PLACES >> (3 * (2 * a + (target[i] >> half_bit)))) & 7
        cell = (place << per_bit) | (b << half_bit) | (target[i] & (half - 1))
        flag = jnp.where(a == 2, 1 << FAR_BIT, 1 << NEAR_BIT)
        flag = jnp.where(i < live, flag, 0)
        index[i] = cell | (pivot[i] << PIVOT_BIT) | (i << SLOT_BIT) | flag
        return 0

    lax.fori_loop(0, slots, word, 0, unroll=16)
    index_copy = pltpu.make_async_copy(index, index_ref, isem.at[3])
    index_copy.start()

    def ready():
        table_copy.wait()
        for pair in pairs:
            for c in pair:
                c.wait()

    sum_cells(0, FAR_BIT, index, listed, total, outs, ready, left, right, table)
    index_copy.wait()


def near_kernel(first, index_ref, table, left, right, *refs):
    *outs, listed, total = refs
    sum_cells(first, NEAR_BIT, index_ref, listed, total, outs, lambda: None, left, right, table)


def cell_shapes(sizes):
    return [jax.ShapeDtypeStruct((n, B, B), bf16) for n in sizes]


def far_sums(sizes, half, owner, target, pivot, count, table, left, right):
    cells = sum(sizes)
    slots = left.shape[0]
    shapes = [jax.ShapeDtypeStruct(x.shape, x.dtype) for x in (left, right, table, pivot)]
    outs = pl.pallas_call(
        functools.partial(far_kernel, half),
        out_shape=cell_shapes(sizes) + shapes,
        in_specs=[HBM] * 3 + [SMEM] + [HBM] * 3,
        out_specs=[VMEM] * (len(sizes) + 3) + [HBM],
        scratch_shapes=[
            pltpu.SMEM((slots,), jnp.int32),
            pltpu.SMEM((slots,), jnp.int32),
            pltpu.SMEM((slots,), jnp.int32),
            pltpu.SMEM((slots,), jnp.int32),
            pltpu.SMEM((slots + UNROLL,), jnp.int32),
            pltpu.VMEM((cells + 1, B, B), bf16),
            pltpu.SemaphoreType.DMA((CHUNKS,)),
            pltpu.SemaphoreType.DMA((CHUNKS,)),
            pltpu.SemaphoreType.DMA,
            pltpu.SemaphoreType.DMA((4,)),
        ],
        compiler_params=pltpu.CompilerParams(vmem_limit_bytes=9 * MIB + cells * 4 * B * B),
        cost_estimate=pl.CostEstimate(
            flops=slots * B**3, bytes_accessed=slots * 8 * B * B + cells * 2 * B * B, transcendentals=0
        ),
        name="far_sums",
    )(stay(owner), stay(target), stay(pivot), count, stay(table), stay(left), stay(right))
    return outs[: len(sizes)], outs[len(sizes) : -1], outs[-1]


def near_sums(first, sizes, index, held):
    left, right, table = held
    cells = sum(sizes)
    slots = left.shape[0]
    return pl.pallas_call(
        functools.partial(near_kernel, first),
        out_shape=cell_shapes(sizes),
        in_specs=[SMEM, VMEM, VMEM, VMEM],
        out_specs=[VMEM] * len(sizes),
        scratch_shapes=[pltpu.SMEM((slots + UNROLL,), jnp.int32), pltpu.VMEM((cells + 1, B, B), bf16)],
        compiler_params=pltpu.CompilerParams(vmem_limit_bytes=9 * MIB + cells * 4 * B * B),
        cost_estimate=pl.CostEstimate(
            flops=slots * 3 * B**3, bytes_accessed=slots * 4 * B * B + cells * 2 * B * B, transcendentals=0
        ),
        name="near_sums",
    )(index, table, left, right)


def local_kernel(index_ref, table_ref, coupling_ref, left_ref, right_ref, diag_ref, seed_ref, *refs):
    base_ref, keep_ref, give_ref, held, left, right, table, lsem, rsem, tsem = refs[-10:]
    slots = left.shape[0]
    rows = coupling_ref.shape[0]
    half = rows // 2
    core = lax.axis_index("section") % 2
    table_copy = pltpu.make_async_copy(table_ref, table, tsem)
    table_copy.start()
    pairs = bulk(left_ref, right_ref, left, right, lsem, rsem)
    for r in range(rows):
        base_ref[r] = coupling_ref[r].astype(f32)

    def offset(r, _):
        dh, dl = split(diag_ref[r])
        sh, sl = split(seed_ref[r])
        o = mm_nt(sh, dh) + (mm_nt(sh, dl) + mm_nt(sl, dh))
        held[(r + core * half) % rows] = o.astype(bf16)
        return 0

    lax.fori_loop(0, rows, offset, 0, unroll=4)
    for i in range(half):
        keep_ref[i] = held[i]
        give_ref[i] = held[half + i]
    table_copy.wait()
    per = slots // CHUNKS
    for k, pair in enumerate(pairs):
        for c in pair:
            c.wait()

        def work(i, _, k=k):
            at = [k * per + i * UNROLL + u for u in range(UNROLL)]
            words = [index_ref[j] for j in at]
            scaled = [mm(left[j], table[(w >> PIVOT_BIT) & 3]).astype(bf16) for j, w in zip(at, words)]
            updates = [mm(x, right[j]).astype(bf16).astype(f32) for x, j in zip(scaled, at)]
            for w, u in zip(words, updates):
                t = w & CELL_MASK
                base_ref[t] = base_ref[t] - u
            return 0

        lax.fori_loop(0, per // UNROLL, work, 0)


def local_and_offset(index, table, coupling, left, right, diag, seed, order):
    slots = left.shape[0]
    rows = coupling.shape[0]
    return pl.pallas_call(
        local_kernel,
        out_shape=[jax.ShapeDtypeStruct((rows, B, B), f32)] + [jax.ShapeDtypeStruct((rows // 2, B, B), bf16)] * 2,
        in_specs=[SMEM, HBM, VMEM, HBM, HBM, VMEM, VMEM] + [ANY] * len(order),
        out_specs=[VMEM] * 3,
        scratch_shapes=[
            pltpu.VMEM((rows, B, B), bf16),
            pltpu.VMEM((slots, B, B), bf16),
            pltpu.VMEM((slots, B, B), bf16),
            pltpu.VMEM(table.shape, bf16),
            pltpu.SemaphoreType.DMA((CHUNKS,)),
            pltpu.SemaphoreType.DMA((CHUNKS,)),
            pltpu.SemaphoreType.DMA,
        ],
        compiler_params=pltpu.CompilerParams(vmem_limit_bytes=16 * MIB),
        cost_estimate=pl.CostEstimate(
            flops=slots * 4 * B**3, bytes_accessed=slots * 4 * B * B + rows * 16 * B * B, transcendentals=0
        ),
        name="local_and_offset",
    )(index, stay(table), coupling, stay(left), stay(right), diag, seed, *order)


def first_totals_kernel(own, *refs):
    arrivals = (refs[2:4], refs[:2])
    outs = refs[-SIDE:]
    h = own.shape[0] // (2 * SIDE)
    for half in range(2):
        for b in range(SIDE):
            t = own[pl.ds((half * SIDE + b) * h, h)].astype(f32)
            for a in arrivals[half]:
                t = t + a[pl.ds(b * h, h)].astype(f32)
            outs[b][pl.ds(half * h, h)] = t.astype(bf16)


def first_totals(own, arrivals, order):
    rows = own.shape[0] // SIDE
    return pl.pallas_call(
        first_totals_kernel,
        out_shape=[jax.ShapeDtypeStruct((rows, B, B), bf16)] * SIDE,
        in_specs=[VMEM] * 5 + [ANY] * len(order),
        out_specs=[VMEM] * SIDE,
        compiler_params=pltpu.CompilerParams(vmem_limit_bytes=9 * MIB),
        cost_estimate=pl.CostEstimate(flops=0, bytes_accessed=256 * 2 * B * B, transcendentals=0),
        name="first_totals",
    )(own, *arrivals, *order)


def coupling_kernel(base_ref, diag_ref, *refs):
    parts = refs[:SIDE]
    new_ref, keep_ref, give_ref, new, held, sem = refs[4:]
    rows = base_ref.shape[0]
    half = rows // 2
    group = half // 2
    core = lax.axis_index("section") % 2
    copies = []
    for g in range(rows // group):

        def finish(i, _, g=g):
            r = g * group + i
            t = base_ref[r]
            for p in parts:
                t = t - p[r].astype(f32)
            new[r] = t
            th, tl = split(t)
            dh, dl = split(diag_ref[r])
            held[(r + core * half) % rows] = -(mm(dh, th) + (mm(dh, tl) + mm(dl, th))).astype(bf16)
            return 0

        lax.fori_loop(0, group, finish, 0, unroll=True)
        part = pl.ds(g * group, group)
        copies.append(pltpu.make_async_copy(new.at[part], new_ref.at[part], sem.at[g]))
        copies[-1].start()
    for i in range(half):
        keep_ref[i] = held[i]
        give_ref[i] = held[half + i]
    for c in copies:
        c.wait()


def coupling_and_step(base, diag, parts):
    rows = base.shape[0]
    half = rows // 2
    return pl.pallas_call(
        coupling_kernel,
        out_shape=[jax.ShapeDtypeStruct((rows, B, B), f32)] + cell_shapes([half, half]),
        in_specs=[VMEM] * (2 + SIDE),
        out_specs=[HBM, VMEM, VMEM],
        scratch_shapes=[
            pltpu.VMEM((rows, B, B), f32),
            pltpu.VMEM((rows, B, B), bf16),
            pltpu.SemaphoreType.DMA((4,)),
        ],
        compiler_params=pltpu.CompilerParams(vmem_limit_bytes=9 * MIB),
        cost_estimate=pl.CostEstimate(flops=rows * 6 * B**3, bytes_accessed=rows * 22 * B * B, transcendentals=0),
        name="coupling_and_step",
    )(base, diag, *parts)


def compose_kernel(chips, keep_ref, offset_ref, got_ref, got_offset_ref, *outs):
    section = lax.axis_index("section")
    chip = section // 2
    half = keep_ref.shape[0]
    per = half // chips

    def compose(first):
        for k in range(chips):
            for j in range(per):
                i = (chip + k) % chips * per + j
                mine = (keep_ref[i], offset_ref[i])
                other = (got_ref[i], got_offset_ref[i])
                (ma, oa), (mb, ob) = (mine, other) if first else (other, mine)
                outs[k][j] = mm(ma, mb).astype(bf16)
                outs[k][per + j] = (oa.astype(f32) + mm_nt(ob, ma)).astype(bf16)

    @pl.when(section % 2 == 0)
    def _():
        compose(True)

    @pl.when(section % 2 == 1)
    def _():
        compose(False)


def compose(chips, keep, offsets, got, got_offsets):
    half = keep.shape[0]
    return pl.pallas_call(
        functools.partial(compose_kernel, chips),
        out_shape=[jax.ShapeDtypeStruct((2 * half // chips, B, B), bf16)] * chips,
        in_specs=[VMEM] * 4,
        out_specs=[VMEM] * chips,
        compiler_params=pltpu.CompilerParams(vmem_limit_bytes=4 * MIB),
        cost_estimate=pl.CostEstimate(flops=half * 4 * B**3, bytes_accessed=half * 12 * B * B, transcendentals=0),
        name="compose",
    )(keep, offsets, got, got_offsets)


def chain_kernel(chips, *refs):
    parts = refs[:chips]
    outs = refs[chips : 2 * chips]
    maps, incoming = refs[2 * chips :]
    chip = lax.axis_index("section") // 2
    per = outs[0].shape[0]
    for part, k in zip(parts, ORDER):
        for i in range(2 * per):
            maps[(chip - k + chips) % chips, i] = part[i]
    current = [jnp.zeros((B, B), f32)] * per
    for c in range(chips - 1, -1, -1):
        for j in range(per):
            incoming[c, j] = current[j].astype(bf16)
            if c > 0:
                new = maps[c, per + j].astype(f32)
                if c < chips - 1:
                    high, low = split(current[j])
                    new = new + (mm_nt(high, maps[c, j]) + mm_nt(low, maps[c, j]))
                current[j] = new
    for k in range(chips):
        for j in range(per):
            outs[k][j] = incoming[(chip + k) % chips, j]


def run_chains(parts):
    chips = len(parts)
    per = parts[0].shape[0] // 2
    return pl.pallas_call(
        functools.partial(chain_kernel, chips),
        out_shape=[jax.ShapeDtypeStruct((per, B, B), bf16)] * chips,
        in_specs=[VMEM] * chips,
        out_specs=[VMEM] * chips,
        scratch_shapes=[pltpu.VMEM((chips, 2 * per, B, B), bf16), pltpu.VMEM((chips, per, B, B), bf16)],
        compiler_params=pltpu.CompilerParams(vmem_limit_bytes=4 * MIB),
        cost_estimate=pl.CostEstimate(
            flops=chips * per * 4 * B**3, bytes_accessed=chips * per * 6 * B * B, transcendentals=0
        ),
        name="run_chains",
    )(*parts)


def expand_kernel(chips, keep_ref, offset_ref, got_ref, got_offset_ref, *refs):
    parts = refs[:chips]
    mine_ref, other_ref = refs[chips:]
    section = lax.axis_index("section")
    chip = section // 2
    half = keep_ref.shape[0]
    per = half // chips

    def expand(first):
        for part, k in zip(parts, ORDER):
            for j in range(per):
                i = (chip - k + chips) % chips * per + j
                mine = (keep_ref[i], offset_ref[i])
                other = (got_ref[i], got_offset_ref[i])
                (ma, oa), (mb, ob) = (mine, other) if first else (other, mine)
                b = ob.astype(f32) + mm_nt(part[j], mb)
                a = oa.astype(f32) + mm_nt(b.astype(bf16), ma)
                mine_ref[i] = a if first else b
                other_ref[i] = (b if first else a).astype(bf16)

    @pl.when(section % 2 == 0)
    def _():
        expand(True)

    @pl.when(section % 2 == 1)
    def _():
        expand(False)


def expand(keep, offsets, got, got_offsets, parts):
    chips = len(parts)
    half = keep.shape[0]
    return pl.pallas_call(
        functools.partial(expand_kernel, chips),
        out_shape=[jax.ShapeDtypeStruct((half, B, B), f32), jax.ShapeDtypeStruct((half, B, B), bf16)],
        in_specs=[VMEM] * (4 + chips),
        out_specs=[VMEM] * 2,
        compiler_params=pltpu.CompilerParams(vmem_limit_bytes=4 * MIB),
        cost_estimate=pl.CostEstimate(flops=half * 6 * B**3, bytes_accessed=half * 16 * B * B, transcendentals=0),
        name="expand",
    )(keep, offsets, got, got_offsets, *parts)


def store_kernel(mine_ref, out_ref, sem):
    half = mine_ref.shape[0]
    core = lax.axis_index("section") % 2
    copy = pltpu.make_async_copy(mine_ref, out_ref.at[pl.ds(core * half, half)], sem)
    copy.start()
    copy.wait()


def store_rows(mine):
    half = mine.shape[0]
    return pl.pallas_call(
        store_kernel,
        out_shape=jax.ShapeDtypeStruct((2 * half, B, B), f32),
        in_specs=[VMEM],
        out_specs=HBM,
        scratch_shapes=[pltpu.SemaphoreType.DMA],
        compiler_params=pltpu.CompilerParams(vmem_limit_bytes=2 * MIB),
        cost_estimate=pl.CostEstimate(flops=0, bytes_accessed=half * 8 * B * B, transcendentals=0),
        name="store_rows",
    )(mine)


def add_kernel(got_ref, part_ref, out_ref, held, sem):
    half = got_ref.shape[0]
    group = half // 2
    core = lax.axis_index("section") % 2
    copies = []
    for g in range(2):
        for i in range(g * group, (g + 1) * group):
            held[i] = got_ref[i].astype(f32)
        to = out_ref.at[pl.ds((1 - core) * half + g * group, group)]
        copies.append(pltpu.make_async_copy(held.at[pl.ds(g * group, group)], to, sem.at[g]))
        copies[-1].start()
    for c in copies:
        c.wait()


def add_rows(got, part):
    half = got.shape[0]
    return pl.pallas_call(
        add_kernel,
        out_shape=jax.ShapeDtypeStruct(part.shape, f32),
        in_specs=[VMEM, HBM],
        out_specs=HBM,
        scratch_shapes=[pltpu.VMEM((half, B, B), f32), pltpu.SemaphoreType.DMA((2,))],
        input_output_aliases={1: 0},
        compiler_params=pltpu.CompilerParams(vmem_limit_bytes=4 * MIB),
        cost_estimate=pl.CostEstimate(flops=0, bytes_accessed=half * 6 * B * B, transcendentals=0),
        name="add_rows",
    )(got, part)


def moved(x, stage, by, sections):
    pairs = []
    for s in range(sections):
        for a in range(SIDE):
            for c in range(SIDE):
                if (s + stage) % 2 == 0:
                    to = (a + by) % SIDE * SIDE + c
                else:
                    to = a * SIDE + (c + by) % SIDE
                pairs.append((s * SIDE * SIDE + a * SIDE + c, s * SIDE * SIDE + to))
    return lax.ppermute(x, ("section", "row"), pairs)


def across(x, sections, by):
    return lax.ppermute(x, "section", [(i, (i + 2 * by) % sections) for i in range(sections)])


def partner(x, sections):
    return lax.ppermute(x, "section", [(i, i ^ 1) for i in range(sections)])


def add(a, b):
    return (a.astype(f32) + b.astype(f32)).astype(bf16)


def per_device(
    coupling,
    diag_inverse,
    pivot_inverse,
    cross_left,
    cross_right,
    cross_pivot,
    cross_owner,
    foreign_target_row,
    cross_count,
    local_left,
    local_right,
    local_pivot,
    local_target,
    adjoint_seed,
):
    sections = lax.axis_size("section")
    rows = coupling.shape[0]
    half = rows // 2
    n = SIDE * half
    group = 2 * n
    local_word = local_target | (local_pivot << PIVOT_BIT)

    far, on_chip, word = far_sums(
        [n] * 2,
        half,
        cross_owner[:, 0],
        foreign_target_row,
        cross_pivot,
        cross_count,
        pivot_inverse,
        cross_left,
        cross_right,
    )
    near = near_sums(group, [n] * 4 + [2 * n], word, on_chip)
    minus_in, plus_in = [], []
    for arrived, k, by in ((minus_in, 1, -1), (plus_in, 0, 1)):
        far_in = moved(far[k], 0, by, sections)
        arrived.append(moved(near[k], 0, by, sections))
        joined = add(near[2 + k], far_in)
        arrived += [moved(joined, 0, by, sections), joined]

    base, offsets, give_offsets = local_and_offset(
        local_word, pivot_inverse, coupling, local_left, local_right, diag_inverse, adjoint_seed, [minus_in[2], plus_in[2]]
    )
    got_offsets = partner(give_offsets, sections)

    arrivals = (minus_in[1], plus_in[0], minus_in[0], plus_in[1])
    totals = first_totals(near[4], arrivals, [base, got_offsets])
    parts = [totals[0]] + [moved(totals[k], 1, k, sections) for k in (2, 1, 3)]
    updated, keep, give = coupling_and_step(base, diag_inverse, parts)
    chips = sections // 2
    got = partner(give, sections)
    maps = compose(chips, keep, offsets, got, got_offsets)
    maps = [across(maps[k], sections, k) if k else maps[0] for k in ORDER]
    incoming = run_chains(maps)
    incoming = [across(incoming[k], sections, k) if k else incoming[0] for k in ORDER]
    mine, other = expand(keep, offsets, got, got_offsets, incoming)
    adjoint = add_rows(partner(other, sections), store_rows(mine))
    return (updated, adjoint)


def solution(mesh):
    spread = ("section", "row")
    block = P(spread, None, None)
    line = P(spread)
    return jax.shard_map(
        per_device,
        mesh=mesh,
        in_specs=(
            block,
            block,
            block,
            block,
            block,
            line,
            P(spread, None),
            line,
            line,
            block,
            block,
            line,
            line,
            block,
        ),
        out_specs=(block, block),
        check_vma=False,
    )
```

profile of v0, /device:TPU:1, one launch (start us, length us, event | category | flops | bytes accessed | tf_op | source)
XLA Modules:
  0.0 90.3 jit_solution(17776644854306510408)
XLA Ops:
  1.3 4.3 %far_sums.1 = (bf16[32,128,128]{2,1,0:T(8,128)(2,1)S(1)}, bf16[32,128,128]{2,1,0:T(8,128)(2,1)S(1)}, bf16[128,128,128]{2,1,0:T(8,128)(2,1)S(1)}, bf16[128,128,12...) custom-call(s32[128]{0:T(128)} %bitcast.1, s32[128]{0:T(128)} %target_ref.1, s32[128]{0:T(128)} %pivot_ref.1, ...), custom_call_target="tpu_custom_call" | custom-call | flops 268435456 | bytes 18874368 | tf_op jit(solution)/shard_map/far_sums/pallas_call | solution.py:163
  5.5 2.5 %collective-permute-start.1 = (bf16[32,128,128]{2,1,0:T(8,128)(2,1)S(1)}, bf16[32,128,128]{2,1,0:T(8,128)(2,1)S(1)}, u32[]{:S(2)}, u32[]{:S(2)}) collective-permute-start(bf16[32,128,128]{2,1,0:T(8,128)(2,1)S(1)} %get-tuple-element.40), channel_id=1, source_target_pairs={{0,4},{1,5},{2,6},{3,7},{4,8},{5,9},{6,10},{7,11},{8,12},{9,13},{1... | collective-permute-start | bytes 3145736 | tf_op jit(solution)/shard_map/ppermute | solution.py:534
  8.1 2.7 %collective-permute-start = (bf16[32,128,128]{2,1,0:T(8,128)(2,1)S(1)}, bf16[32,128,128]{2,1,0:T(8,128)(2,1)S(1)}, u32[]{:S(2)}, u32[]{:S(2)}) collective-permute-start(bf16[32,128,128]{2,1,0:T(8,128)(2,1)S(1)} %get-tuple-element.38), channel_id=1, source_target_pairs={{0,12},{1,13},{2,14},{3,15},{4,0},{5,1},{6,2},{7,3},{8,4},{9,5},{1... | collective-permute-start | bytes 3145736 | tf_op jit(solution)/shard_map/ppermute | solution.py:534
  10.7 3.1 %near_sums.1 = (bf16[32,128,128]{2,1,0:T(8,128)(2,1)S(1)}, bf16[32,128,128]{2,1,0:T(8,128)(2,1)S(1)}, bf16[32,128,128]{2,1,0:T(8,128)(2,1)S(1)}, bf16[32,128,128...) custom-call(s32[128]{0:T(128)S(1)} %get-tuple-element.33.index_ref, bf16[4,128,128]{2,1,0:T(8,128)(2,1)S(1)} %get-tuple-element.34.table, ...), custom_call_target="tpu_custom_call" | custom-call | flops 805306368 | bytes 14680064 | tf_op jit(solution)/shard_map/near_sums/pallas_call | solution.py:193
  13.8 0.1 collective-permute-start.3
  13.9 3.8 %collective-permute-start.4 = (bf16[32,128,128]{2,1,0:T(8,128)(2,1)S(1)}, bf16[32,128,128]{2,1,0:T(8,128)(2,1)S(1)}, u32[]{:S(2)}, u32[]{:S(2)}) collective-permute-start(bf16[32,128,128]{2,1,0:T(8,128)(2,1)S(1)} %get-tuple-element.44), channel_id=1, source_target_pairs={{0,12},{1,13},{2,14},{3,15},{4,0},{5,1},{6,2},{7,3},{8,4},{9,5},{1... | collective-permute-start | bytes 3145736 | tf_op jit(solution)/shard_map/ppermute | solution.py:534
  17.7 5.4 %collective-permute-done.1 = bf16[32,128,128]{2,1,0:T(8,128)(2,1)S(1)} collective-permute-done((bf16[32,128,128]{2,1,0:T(8,128)(2,1)S(1)}, bf16[32,128,128]{2,1,0:T(8,128)(2,1)S(1)}, u32[]{:S(2)}, u32[]{:S(2)}) %collective-permute-start.1) | collective-permute-done | bytes 1048608 | tf_op jit(solution)/shard_map/ppermute | solution.py:534
  23.1 0.4 add_convert_fusion.refs_1_
  23.5 0.0 copy-start.3
  23.5 0.0 copy-start.4
  23.5 0.0 copy-start
  23.6 0.0 copy-start.1
  23.6 0.0 copy-start.2
  23.6 0.1 collective-permute-start.5
  23.7 0.0 collective-permute-done
  23.7 0.5 add_convert_fusion.1.refs_0_
  24.1 2.7 %collective-permute-start.2 = (bf16[32,128,128]{2,1,0:T(8,128)(2,1)S(1)}, bf16[32,128,128]{2,1,0:T(8,128)(2,1)S(1)}, u32[]{:S(2)}, u32[]{:S(2)}) collective-permute-start(bf16[32,128,128]{2,1,0:T(8,128)(2,1)S(1)} %add_convert_fusion.1.refs_0_), channel_id=1, source_target_pairs={{0,12},{1,13},{2,14},{3,15},{4,0},{5,1},{6,2},{7,3},{8,4},{9,5},{1... | collective-permute-start | bytes 3145736 | tf_op jit(solution)/shard_map/ppermute | solution.py:534
  26.9 7.4 %local_and_offset.1 = (f32[16,128,128]{2,1,0:T(8,128)S(1)}, bf16[8,128,128]{2,1,0:T(8,128)(2,1)S(1)}, bf16[8,128,128]{2,1,0:T(8,128)(2,1)S(1)}) custom-call(s32[128]{0:T(128)S(1)} %shift-left_or_fusion.index_ref, bf16[4,128,128]{2,1,0:T(8,128)(2,1)} %table_ref.3, bf16[16,128,128]{2,1,0:T(8,128)(2,1)S(1)} %copy-done.2, bf16[128,128,128]{2,1,0:T(8,128)(2,1)} %left_ref.3, ...), custom_call_target="tpu_custom_call" | custom-call | flops 1073741824 | bytes 12582912 | tf_op jit(solution)/shard_map/local_and_offset/pallas_call | solution.py:252
  34.3 1.1 %collective-permute-start.6 = (bf16[8,128,128]{2,1,0:T(8,128)(2,1)S(1)}, bf16[8,128,128]{2,1,0:T(8,128)(2,1)S(1)}, u32[]{:S(2)}, u32[]{:S(2)}) collective-permute-start(bf16[8,128,128]{2,1,0:T(8,128)(2,1)S(1)} %get-tuple-element.45), channel_id=1, source_target_pairs={{0,16},{16,0},{32,48},{48,32},{64,80},{80,64},{96,112},{112,96},{1... | collective-permute-start | bytes 786440 | tf_op jit(solution)/shard_map/ppermute | solution.py:542
  35.3 0.0 collective-permute-done.3.refs_1_
  35.3 0.0 collective-permute-done.4.refs_2_
  35.3 1.2 %collective-permute-done.6.refs_5_.got_offset_ref = bf16[8,128,128]{2,1,0:T(8,128)(2,1)S(1)} collective-permute-done((bf16[8,128,128]{2,1,0:T(8,128)(2,1)S(1)}, bf16[8,128,128]{2,1,0:T(8,128)(2,1)S(1)}, u32[]{:S(2)}, u32[]{:S(2)}) %collective-permute-start.6) | collective-permute-done | bytes 262176 | tf_op jit(solution)/shard_map/ppermute | solution.py:542
  36.5 9.1 %collective-permute-done.5.refs_3_ = bf16[32,128,128]{2,1,0:T(8,128)(2,1)S(1)} collective-permute-done((bf16[32,128,128]{2,1,0:T(8,128)(2,1)S(1)}, bf16[32,128,128]{2,1,0:T(8,128)(2,1)S(1)}, u32[]{:S(2)}, u32[]{:S(2)}) %collective-permute-start.5) | collective-permute-done | bytes 1048608 | tf_op jit(solution)/shard_map/ppermute | solution.py:534
  45.6 0.7 first_totals.1
  46.4 2.8 %collective-permute-start.7 = (bf16[16,128,128]{2,1,0:T(8,128)(2,1)S(1)}, bf16[16,128,128]{2,1,0:T(8,128)(2,1)S(1)}, u32[]{:S(2)}, u32[]{:S(2)}) collective-permute-start(bf16[16,128,128]{2,1,0:T(8,128)(2,1)S(1)} %get-tuple-element.47), channel_id=1, source_target_pairs={{0,2},{1,3},{2,0},{3,1},{4,6},{5,7},{6,4},{7,5},{8,10},{9,11},{10,... | collective-permute-start | bytes 1572872 | tf_op jit(solution)/shard_map/ppermute | solution.py:534
  49.2 2.7 %collective-permute-start.9 = (bf16[16,128,128]{2,1,0:T(8,128)(2,1)S(1)}, bf16[16,128,128]{2,1,0:T(8,128)(2,1)S(1)}, u32[]{:S(2)}, u32[]{:S(2)}) collective-permute-start(bf16[16,128,128]{2,1,0:T(8,128)(2,1)S(1)} %get-tuple-element.49), channel_id=1, source_target_pairs={{0,3},{1,0},{2,1},{3,2},{4,7},{5,4},{6,5},{7,6},{8,11},{9,8},{10,9... | collective-permute-start | bytes 1572872 | tf_op jit(solution)/shard_map/ppermute | solution.py:534
  51.9 4.5 %collective-permute-done.7.refs_1_ = bf16[16,128,128]{2,1,0:T(8,128)(2,1)S(1)} collective-permute-done((bf16[16,128,128]{2,1,0:T(8,128)(2,1)S(1)}, bf16[16,128,128]{2,1,0:T(8,128)(2,1)S(1)}, u32[]{:S(2)}, u32[]{:S(2)}) %collective-permute-start.7) | collective-permute-done | bytes 524320 | tf_op jit(solution)/shard_map/ppermute | solution.py:534
  56.3 5.6 %collective-permute-done.8.refs_2_ = bf16[16,128,128]{2,1,0:T(8,128)(2,1)S(1)} collective-permute-done((bf16[16,128,128]{2,1,0:T(8,128)(2,1)S(1)}, bf16[16,128,128]{2,1,0:T(8,128)(2,1)S(1)}, u32[]{:S(2)}, u32[]{:S(2)}) %collective-permute-start.8) | collective-permute-done | bytes 524320 | tf_op jit(solution)/shard_map/ppermute | solution.py:534
  61.9 1.6 %coupling_and_step.1 = (f32[16,128,128]{2,1,0:T(8,128)}, bf16[8,128,128]{2,1,0:T(8,128)(2,1)S(1)}, bf16[8,128,128]{2,1,0:T(8,128)(2,1)S(1)}) custom-call(f32[16,128,128]{2,1,0:T(8,128)S(1)} %get-tuple-element.41.refs_4_.base_ref, f32[16,128,128]{2,1,0:T(8,128)S(1)} %copy-done, bf16[16,128,128]{2,1,0:T(8,128)(2,1)S(1)} %get-tuple-element.46.refs_0_, ...), custom_call_target="tpu_custom_call" | custom-call | flops 201326592 | bytes 5767168 | tf_op jit(solution)/shard_map/coupling_and_step/pallas_call | solution.py:334
  63.5 2.8 %collective-permute-start.10 = (bf16[8,128,128]{2,1,0:T(8,128)(2,1)S(1)}, bf16[8,128,128]{2,1,0:T(8,128)(2,1)S(1)}, u32[]{:S(2)}, u32[]{:S(2)}) collective-permute-start(bf16[8,128,128]{2,1,0:T(8,128)(2,1)S(1)} %get-tuple-element.53), channel_id=1, source_target_pairs={{0,16},{16,0},{32,48},{48,32},{64,80},{80,64},{96,112},{112,96},{1... | collective-permute-start | bytes 786440 | tf_op jit(solution)/shard_map/ppermute | solution.py:542
  66.3 1.2 %collective-permute-done.10.got_ref = bf16[8,128,128]{2,1,0:T(8,128)(2,1)S(1)} collective-permute-done((bf16[8,128,128]{2,1,0:T(8,128)(2,1)S(1)}, bf16[8,128,128]{2,1,0:T(8,128)(2,1)S(1)}, u32[]{:S(2)}, u32[]{:S(2)}) %collective-permute-start.10) | collective-permute-done | bytes 262176 | tf_op jit(solution)/shard_map/ppermute | solution.py:542
  67.5 0.4 compose.1
  67.9 3.3 %collective-permute-start.11 = (bf16[4,128,128]{2,1,0:T(8,128)(2,1)S(1)}, bf16[4,128,128]{2,1,0:T(8,128)(2,1)S(1)}, u32[]{:S(2)}, u32[]{:S(2)}) collective-permute-start(bf16[4,128,128]{2,1,0:T(8,128)(2,1)S(1)} %get-tuple-element.55), channel_id=1, source_target_pairs={{0,64},{16,80},{32,96},{48,112},{64,0},{80,16},{96,32},{112,48},{1... | collective-permute-start | bytes 393224 | tf_op jit(solution)/shard_map/ppermute | solution.py:538
  71.1 0.4 collective-permute-start.12
  71.5 2.3 %collective-permute-start.13 = (bf16[4,128,128]{2,1,0:T(8,128)(2,1)S(1)}, bf16[4,128,128]{2,1,0:T(8,128)(2,1)S(1)}, u32[]{:S(2)}, u32[]{:S(2)}) collective-permute-start(bf16[4,128,128]{2,1,0:T(8,128)(2,1)S(1)} %get-tuple-element.57), channel_id=1, source_target_pairs={{0,96},{16,112},{32,0},{48,16},{64,32},{80,48},{96,64},{112,80},{1... | collective-permute-start | bytes 393224 | tf_op jit(solution)/shard_map/ppermute | solution.py:538
  73.8 0.6 collective-permute-done.11.refs_1_
  74.4 3.0 %collective-permute-done.12.refs_2_ = bf16[4,128,128]{2,1,0:T(8,128)(2,1)S(1)} collective-permute-done((bf16[4,128,128]{2,1,0:T(8,128)(2,1)S(1)}, bf16[4,128,128]{2,1,0:T(8,128)(2,1)S(1)}, u32[]{:S(2)}, u32[]{:S(2)}) %collective-permute-start.12) | collective-permute-done | bytes 131104 | tf_op jit(solution)/shard_map/ppermute | solution.py:538
  77.4 0.4 run_chains.1
  77.9 2.0 %collective-permute-start.14 = (bf16[2,128,128]{2,1,0:T(8,128)(2,1)S(1)}, bf16[2,128,128]{2,1,0:T(8,128)(2,1)S(1)}, u32[]{:S(2)}, u32[]{:S(2)}) collective-permute-start(bf16[2,128,128]{2,1,0:T(8,128)(2,1)S(1)} %get-tuple-element.59), channel_id=1, source_target_pairs={{0,64},{16,80},{32,96},{48,112},{64,0},{80,16},{96,32},{112,48},{1... | collective-permute-start | bytes 196616 | tf_op jit(solution)/shard_map/ppermute | solution.py:538
  79.8 1.4 %collective-permute-start.15 = (bf16[2,128,128]{2,1,0:T(8,128)(2,1)S(1)}, bf16[2,128,128]{2,1,0:T(8,128)(2,1)S(1)}, u32[]{:S(2)}, u32[]{:S(2)}) collective-permute-start(bf16[2,128,128]{2,1,0:T(8,128)(2,1)S(1)} %get-tuple-element.60), channel_id=1, source_target_pairs={{0,32},{16,48},{32,64},{48,80},{64,96},{80,112},{96,0},{112,16},{1... | collective-permute-start | bytes 196616 | tf_op jit(solution)/shard_map/ppermute | solution.py:538
  81.3 1.3 %collective-permute-start.16 = (bf16[2,128,128]{2,1,0:T(8,128)(2,1)S(1)}, bf16[2,128,128]{2,1,0:T(8,128)(2,1)S(1)}, u32[]{:S(2)}, u32[]{:S(2)}) collective-permute-start(bf16[2,128,128]{2,1,0:T(8,128)(2,1)S(1)} %get-tuple-element.61), channel_id=1, source_target_pairs={{0,96},{16,112},{32,0},{48,16},{64,32},{80,48},{96,64},{112,80},{1... | collective-permute-start | bytes 196616 | tf_op jit(solution)/shard_map/ppermute | solution.py:538
  82.5 0.1 collective-permute-done.14.refs_1_
  82.6 2.5 %collective-permute-done.15.refs_2_ = bf16[2,128,128]{2,1,0:T(8,128)(2,1)S(1)} collective-permute-done((bf16[2,128,128]{2,1,0:T(8,128)(2,1)S(1)}, bf16[2,128,128]{2,1,0:T(8,128)(2,1)S(1)}, u32[]{:S(2)}, u32[]{:S(2)}) %collective-permute-start.15) | collective-permute-done | bytes 65568 | tf_op jit(solution)/shard_map/ppermute | solution.py:538
  85.1 0.5 expand.1
  85.6 2.5 %collective-permute-start.17 = (bf16[8,128,128]{2,1,0:T(8,128)(2,1)S(1)}, bf16[8,128,128]{2,1,0:T(8,128)(2,1)S(1)}, u32[]{:S(2)}, u32[]{:S(2)}) collective-permute-start(bf16[8,128,128]{2,1,0:T(8,128)(2,1)S(1)} %get-tuple-element.62), channel_id=1, source_target_pairs={{0,16},{16,0},{32,48},{48,32},{64,80},{80,64},{96,112},{112,96},{1... | collective-permute-start | bytes 786440 | tf_op jit(solution)/shard_map/ppermute | solution.py:542
  88.1 0.8 store_rows.1.part_ref
  88.9 0.4 collective-permute-done.17.got_ref
  89.3 0.8 add_rows.1
  (11 shorter events, 0.0 us)
Async XLA Ops:
  5.5 17.6 %collective-permute-start.1 = (bf16[32,128,128]{2,1,0:T(8,128)(2,1)S(1)}, bf16[32,128,128]{2,1,0:T(8,128)(2,1)S(1)}, u32[]{:S(2)}, u32[]{:S(2)}) collective-permute-start(bf16[32,128,128]{2,1,0:T(8,128)(2,1)S(1)} %get-tuple-element.40), channel_id=1, source_target_pairs={{0,4},{1,5},{2,6},{3,7},{4,8},{5,9},{6,10},{7,11},{8,12},{9,13},{1... | collective-permute-start | bytes 3145736 | tf_op jit(solution)/shard_map/ppermute | solution.py:534
  8.1 15.6 %collective-permute-start = (bf16[32,128,128]{2,1,0:T(8,128)(2,1)S(1)}, bf16[32,128,128]{2,1,0:T(8,128)(2,1)S(1)}, u32[]{:S(2)}, u32[]{:S(2)}) collective-permute-start(bf16[32,128,128]{2,1,0:T(8,128)(2,1)S(1)} %get-tuple-element.38), channel_id=1, source_target_pairs={{0,12},{1,13},{2,14},{3,15},{4,0},{5,1},{6,2},{7,3},{8,4},{9,5},{1... | collective-permute-start | bytes 3145736 | tf_op jit(solution)/shard_map/ppermute | solution.py:534
  13.8 21.5 %collective-permute-start.3 = (bf16[32,128,128]{2,1,0:T(8,128)(2,1)S(1)}, bf16[32,128,128]{2,1,0:T(8,128)(2,1)S(1)}, u32[]{:S(2)}, u32[]{:S(2)}) collective-permute-start(bf16[32,128,128]{2,1,0:T(8,128)(2,1)S(1)} %get-tuple-element.43), channel_id=1, source_target_pairs={{0,4},{1,5},{2,6},{3,7},{4,8},{5,9},{6,10},{7,11},{8,12},{9,13},{1... | collective-permute-start | bytes 3145736 | tf_op jit(solution)/shard_map/ppermute | solution.py:534
  13.9 21.4 %collective-permute-start.4 = (bf16[32,128,128]{2,1,0:T(8,128)(2,1)S(1)}, bf16[32,128,128]{2,1,0:T(8,128)(2,1)S(1)}, u32[]{:S(2)}, u32[]{:S(2)}) collective-permute-start(bf16[32,128,128]{2,1,0:T(8,128)(2,1)S(1)} %get-tuple-element.44), channel_id=1, source_target_pairs={{0,12},{1,13},{2,14},{3,15},{4,0},{5,1},{6,2},{7,3},{8,4},{9,5},{1... | collective-permute-start | bytes 3145736 | tf_op jit(solution)/shard_map/ppermute | solution.py:534
  23.5 3.3 %copy-start.3 = (s32[128]{0:T(128)S(1)}, s32[128]{0:T(128)}, u32[]{:S(2)}) copy-start(s32[128]{0:T(128)} %param.26) | copy-start | bytes 1540
  23.5 3.3 %copy-start.4 = (s32[128]{0:T(128)S(1)}, s32[128]{0:T(128)}, u32[]{:S(2)}) copy-start(s32[128]{0:T(128)} %param.25) | copy-start | bytes 1540
  23.5 3.3 %copy-start = (f32[16,128,128]{2,1,0:T(8,128)S(1)}, f32[16,128,128]{2,1,0:T(8,128)}, u32[]{:S(2)}) copy-start(f32[16,128,128]{2,1,0:T(8,128)} %diag_ref.3) | copy-start | bytes 3145732
  23.6 3.3 %copy-start.1 = (f32[16,128,128]{2,1,0:T(8,128)S(1)}, f32[16,128,128]{2,1,0:T(8,128)}, u32[]{:S(2)}) copy-start(f32[16,128,128]{2,1,0:T(8,128)} %seed_ref.1) | copy-start | bytes 3145732
  23.6 3.3 %copy-start.2 = (bf16[16,128,128]{2,1,0:T(8,128)(2,1)S(1)}, bf16[16,128,128]{2,1,0:T(8,128)(2,1)}, u32[]{:S(2)}) copy-start(bf16[16,128,128]{2,1,0:T(8,128)(2,1)} %coupling_ref.1) | copy-start | bytes 1572868
  23.6 22.0 %collective-permute-start.5 = (bf16[32,128,128]{2,1,0:T(8,128)(2,1)S(1)}, bf16[32,128,128]{2,1,0:T(8,128)(2,1)S(1)}, u32[]{:S(2)}, u32[]{:S(2)}) collective-permute-start(bf16[32,128,128]{2,1,0:T(8,128)(2,1)S(1)} %add_convert_fusion.refs_1_), channel_id=1, source_target_pairs={{0,4},{1,5},{2,6},{3,7},{4,8},{5,9},{6,10},{7,11},{8,12},{9,13},{1... | collective-permute-start | bytes 3145736 | tf_op jit(solution)/shard_map/ppermute | solution.py:534
  24.1 21.5 %collective-permute-start.2 = (bf16[32,128,128]{2,1,0:T(8,128)(2,1)S(1)}, bf16[32,128,128]{2,1,0:T(8,128)(2,1)S(1)}, u32[]{:S(2)}, u32[]{:S(2)}) collective-permute-start(bf16[32,128,128]{2,1,0:T(8,128)(2,1)S(1)} %add_convert_fusion.1.refs_0_), channel_id=1, source_target_pairs={{0,12},{1,13},{2,14},{3,15},{4,0},{5,1},{6,2},{7,3},{8,4},{9,5},{1... | collective-permute-start | bytes 3145736 | tf_op jit(solution)/shard_map/ppermute | solution.py:534
  34.3 2.2 %collective-permute-start.6 = (bf16[8,128,128]{2,1,0:T(8,128)(2,1)S(1)}, bf16[8,128,128]{2,1,0:T(8,128)(2,1)S(1)}, u32[]{:S(2)}, u32[]{:S(2)}) collective-permute-start(bf16[8,128,128]{2,1,0:T(8,128)(2,1)S(1)} %get-tuple-element.45), channel_id=1, source_target_pairs={{0,16},{16,0},{32,48},{48,32},{64,80},{80,64},{96,112},{112,96},{1... | collective-permute-start | bytes 786440 | tf_op jit(solution)/shard_map/ppermute | solution.py:542
  46.4 10.0 %collective-permute-start.7 = (bf16[16,128,128]{2,1,0:T(8,128)(2,1)S(1)}, bf16[16,128,128]{2,1,0:T(8,128)(2,1)S(1)}, u32[]{:S(2)}, u32[]{:S(2)}) collective-permute-start(bf16[16,128,128]{2,1,0:T(8,128)(2,1)S(1)} %get-tuple-element.47), channel_id=1, source_target_pairs={{0,2},{1,3},{2,0},{3,1},{4,6},{5,7},{6,4},{7,5},{8,10},{9,11},{10,... | collective-permute-start | bytes 1572872 | tf_op jit(solution)/shard_map/ppermute | solution.py:534
  49.2 12.7 %collective-permute-start.8 = (bf16[16,128,128]{2,1,0:T(8,128)(2,1)S(1)}, bf16[16,128,128]{2,1,0:T(8,128)(2,1)S(1)}, u32[]{:S(2)}, u32[]{:S(2)}) collective-permute-start(bf16[16,128,128]{2,1,0:T(8,128)(2,1)S(1)} %get-tuple-element.48), channel_id=1, source_target_pairs={{0,1},{1,2},{2,3},{3,0},{4,5},{5,6},{6,7},{7,4},{8,9},{9,10},{10,1... | collective-permute-start | bytes 1572872 | tf_op jit(solution)/shard_map/ppermute | solution.py:534
  49.2 12.7 %collective-permute-start.9 = (bf16[16,128,128]{2,1,0:T(8,128)(2,1)S(1)}, bf16[16,128,128]{2,1,0:T(8,128)(2,1)S(1)}, u32[]{:S(2)}, u32[]{:S(2)}) collective-permute-start(bf16[16,128,128]{2,1,0:T(8,128)(2,1)S(1)} %get-tuple-element.49), channel_id=1, source_target_pairs={{0,3},{1,0},{2,1},{3,2},{4,7},{5,4},{6,5},{7,6},{8,11},{9,8},{10,9... | collective-permute-start | bytes 1572872 | tf_op jit(solution)/shard_map/ppermute | solution.py:534
  63.5 4.0 %collective-permute-start.10 = (bf16[8,128,128]{2,1,0:T(8,128)(2,1)S(1)}, bf16[8,128,128]{2,1,0:T(8,128)(2,1)S(1)}, u32[]{:S(2)}, u32[]{:S(2)}) collective-permute-start(bf16[8,128,128]{2,1,0:T(8,128)(2,1)S(1)} %get-tuple-element.53), channel_id=1, source_target_pairs={{0,16},{16,0},{32,48},{48,32},{64,80},{80,64},{96,112},{112,96},{1... | collective-permute-start | bytes 786440 | tf_op jit(solution)/shard_map/ppermute | solution.py:542
  67.9 6.6 %collective-permute-start.11 = (bf16[4,128,128]{2,1,0:T(8,128)(2,1)S(1)}, bf16[4,128,128]{2,1,0:T(8,128)(2,1)S(1)}, u32[]{:S(2)}, u32[]{:S(2)}) collective-permute-start(bf16[4,128,128]{2,1,0:T(8,128)(2,1)S(1)} %get-tuple-element.55), channel_id=1, source_target_pairs={{0,64},{16,80},{32,96},{48,112},{64,0},{80,16},{96,32},{112,48},{1... | collective-permute-start | bytes 393224 | tf_op jit(solution)/shard_map/ppermute | solution.py:538
  71.1 6.3 %collective-permute-start.12 = (bf16[4,128,128]{2,1,0:T(8,128)(2,1)S(1)}, bf16[4,128,128]{2,1,0:T(8,128)(2,1)S(1)}, u32[]{:S(2)}, u32[]{:S(2)}) collective-permute-start(bf16[4,128,128]{2,1,0:T(8,128)(2,1)S(1)} %get-tuple-element.56), channel_id=1, source_target_pairs={{0,32},{16,48},{32,64},{48,80},{64,96},{80,112},{96,0},{112,16},{1... | collective-permute-start | bytes 393224 | tf_op jit(solution)/shard_map/ppermute | solution.py:538
  71.5 5.9 %collective-permute-start.13 = (bf16[4,128,128]{2,1,0:T(8,128)(2,1)S(1)}, bf16[4,128,128]{2,1,0:T(8,128)(2,1)S(1)}, u32[]{:S(2)}, u32[]{:S(2)}) collective-permute-start(bf16[4,128,128]{2,1,0:T(8,128)(2,1)S(1)} %get-tuple-element.57), channel_id=1, source_target_pairs={{0,96},{16,112},{32,0},{48,16},{64,32},{80,48},{96,64},{112,80},{1... | collective-permute-start | bytes 393224 | tf_op jit(solution)/shard_map/ppermute | solution.py:538
  77.9 4.7 %collective-permute-start.14 = (bf16[2,128,128]{2,1,0:T(8,128)(2,1)S(1)}, bf16[2,128,128]{2,1,0:T(8,128)(2,1)S(1)}, u32[]{:S(2)}, u32[]{:S(2)}) collective-permute-start(bf16[2,128,128]{2,1,0:T(8,128)(2,1)S(1)} %get-tuple-element.59), channel_id=1, source_target_pairs={{0,64},{16,80},{32,96},{48,112},{64,0},{80,16},{96,32},{112,48},{1... | collective-permute-start | bytes 196616 | tf_op jit(solution)/shard_map/ppermute | solution.py:538
  79.8 5.2 %collective-permute-start.15 = (bf16[2,128,128]{2,1,0:T(8,128)(2,1)S(1)}, bf16[2,128,128]{2,1,0:T(8,128)(2,1)S(1)}, u32[]{:S(2)}, u32[]{:S(2)}) collective-permute-start(bf16[2,128,128]{2,1,0:T(8,128)(2,1)S(1)} %get-tuple-element.60), channel_id=1, source_target_pairs={{0,32},{16,48},{32,64},{48,80},{64,96},{80,112},{96,0},{112,16},{1... | collective-permute-start | bytes 196616 | tf_op jit(solution)/shard_map/ppermute | solution.py:538
  81.3 3.8 %collective-permute-start.16 = (bf16[2,128,128]{2,1,0:T(8,128)(2,1)S(1)}, bf16[2,128,128]{2,1,0:T(8,128)(2,1)S(1)}, u32[]{:S(2)}, u32[]{:S(2)}) collective-permute-start(bf16[2,128,128]{2,1,0:T(8,128)(2,1)S(1)} %get-tuple-element.61), channel_id=1, source_target_pairs={{0,96},{16,112},{32,0},{48,16},{64,32},{80,48},{96,64},{112,80},{1... | collective-permute-start | bytes 196616 | tf_op jit(solution)/shard_map/ppermute | solution.py:538
  85.6 3.7 %collective-permute-start.17 = (bf16[8,128,128]{2,1,0:T(8,128)(2,1)S(1)}, bf16[8,128,128]{2,1,0:T(8,128)(2,1)S(1)}, u32[]{:S(2)}, u32[]{:S(2)}) collective-permute-start(bf16[8,128,128]{2,1,0:T(8,128)(2,1)S(1)} %get-tuple-element.62), channel_id=1, source_target_pairs={{0,16},{16,0},{32,48},{48,32},{64,80},{80,64},{96,112},{112,96},{1... | collective-permute-start | bytes 786440 | tf_op jit(solution)/shard_map/ppermute | solution.py:542
where the time goes:
time: 90.5 us; the launch traced here: 90.3 us
  starting transfers between devices  34.3 us (38%)
  waiting for transfers between devices  33.4 us (37%)
  Pallas kernels  20.1 us (22%)
  between operations  1.62 us (2%)
    ppermute x9, waiting for transfers between devices, moved(): return lax.ppermute(x, ('section', 'row'), pairs)  24.5 us
    ppermute x9, starting transfers between devices, moved(): return lax.ppermute(x, ('section', 'row'), pairs)  17.4 us
    ppermute x6, starting transfers between devices, across(): lax.ppermute(x, 'section', [(i, (i + 2 * by) % sections) for i in range(s...  10.6 us
    pallas_call x1, Pallas kernels, local_and_offset(): pl.pallas_call(local_kernel, out_shape=[jax.ShapeDtypeStruct((rows, B, B)...  7.38 us
    ppermute x3, starting transfers between devices, partner(): return lax.ppermute(x, 'section', [(i, i ^ 1) for i in range(sections)])  6.36 us
    ppermute x6, waiting for transfers between devices, across(): lax.ppermute(x, 'section', [(i, (i + 2 * by) % sections) for i in range(s...  6.16 us
    pallas_call x1, Pallas kernels, far_sums(): pl.pallas_call(functools.partial(far_kernel, half), out_shape=cell_shapes...  4.26 us
    pallas_call x1, Pallas kernels, near_sums(): pl.pallas_call(functools.partial(near_kernel, first), out_shape=cell_shap...  3.1 us
  transfers between devices with their start and end apart: 18, of which 11 were waited for; matrix products, arithmetic and copies ran while one was open for 1% of the time, Pallas kernels for 12%

commit v1 on v0

--- a/solution.py
+++ b/solution.py
@@ -595,7 +595,7 @@
 
     arrivals = (minus_in[1], plus_in[0], minus_in[0], plus_in[1])
     totals = first_totals(near[4], arrivals, [base, got_offsets])
-    parts = [totals[0]] + [moved(totals[k], 1, k, sections) for k in (2, 1, 3)]
+    parts = [totals[0]] + [moved(totals[k], 1, k, sections) for k in (1, 2, 3)]
     updated, keep, give = coupling_and_step(base, diag_inverse, parts)
     chips = sections // 2
     got = partner(give, sections)

time: 90.5 us -> 91.3 us (level)
  starting transfers between devices: 34.3 us -> 30.5 us
  Pallas kernels: 20.1 us -> 22.9 us
  waiting for transfers between devices: 33.4 us -> 35.2 us
    ppermute x9, starting transfers between devices: 17.4 us -> 14.7 us  [moved(): return lax.ppermute(x, ('section', 'row'), pairs)]
    pallas_call x1, Pallas kernels: 3.1 us -> 4.98 us  [near_sums(): pl.pallas_call(functools.partial(near_kernel, first), out_shape=cell_shap...]
    ppermute x9, waiting for transfers between devices: 24.5 us -> 26 us  [moved(): return lax.ppermute(x, ('section', 'row'), pairs)]
    pallas_call x1, Pallas kernels: 4.26 us -> 5.2 us  [far_sums(): pl.pallas_call(functools.partial(far_kernel, half), out_shape=cell_shapes...]
  transfers between devices with their start and end apart: 18 -> 18, of which waited for: 11 -> 10; matrix products, arithmetic and copies ran while one was open for 1% -> 1% of each run, Pallas kernels for 12% -> 14%
where the time goes in v1:
time: 91.3 us; the launch traced here: 91.2 us
  waiting for transfers between devices  35.2 us (39%)
  starting transfers between devices  30.5 us (33%)
  Pallas kernels  22.9 us (25%)
  between operations  1.62 us (2%)
    ppermute x9, waiting for transfers between devices, moved(): return lax.ppermute(x, ('section', 'row'), pairs)  26 us
    ppermute x9, starting transfers between devices, moved(): return lax.ppermute(x, ('section', 'row'), pairs)  14.7 us
    ppermute x6, starting transfers between devices, across(): lax.ppermute(x, 'section', [(i, (i + 2 * by) % sections) for i in range(s...  10.1 us
    pallas_call x1, Pallas kernels, local_and_offset(): pl.pallas_call(local_kernel, out_shape=[jax.ShapeDtypeStruct((rows, B, B)...  7.4 us
    ppermute x6, waiting for transfers between devices, across(): lax.ppermute(x, 'section', [(i, (i + 2 * by) % sections) for i in range(s...  6.59 us
    ppermute x3, starting transfers between devices, partner(): return lax.ppermute(x, 'section', [(i, i ^ 1) for i in range(sections)])  5.76 us
    pallas_call x1, Pallas kernels, far_sums(): pl.pallas_call(functools.partial(far_kernel, half), out_shape=cell_shapes...  5.2 us
    pallas_call x1, Pallas kernels, near_sums(): pl.pallas_call(functools.partial(near_kernel, first), out_shape=cell_shap...  4.98 us
  transfers between devices with their start and end apart: 18, of which 10 were waited for; matrix products, arithmetic and copies ran while one was open for 1% of the time, Pallas kernels for 14%

profile of v1, /device:TPU:1, one launch (start us, length us, event | category | flops | bytes accessed | tf_op | source)
XLA Modules:
  0.0 91.2 jit_solution(17804021810201500914)
XLA Ops:
  1.3 5.2 %far_sums.1 = (bf16[32,128,128]{2,1,0:T(8,128)(2,1)S(1)}, bf16[32,128,128]{2,1,0:T(8,128)(2,1)S(1)}, bf16[128,128,128]{2,1,0:T(8,128)(2,1)S(1)}, bf16[128,128,12...) custom-call(s32[128]{0:T(128)} %bitcast.1, s32[128]{0:T(128)} %target_ref.1, s32[128]{0:T(128)} %pivot_ref.1, ...), custom_call_target="tpu_custom_call" | custom-call | flops 268435456 | bytes 18874368 | tf_op jit(solution)/shard_map/far_sums/pallas_call | solution.py:163
  6.5 2.1 %collective-permute-start.1 = (bf16[32,128,128]{2,1,0:T(8,128)(2,1)S(1)}, bf16[32,128,128]{2,1,0:T(8,128)(2,1)S(1)}, u32[]{:S(2)}, u32[]{:S(2)}) collective-permute-start(bf16[32,128,128]{2,1,0:T(8,128)(2,1)S(1)} %get-tuple-element.40), channel_id=1, source_target_pairs={{0,4},{1,5},{2,6},{3,7},{4,8},{5,9},{6,10},{7,11},{8,12},{9,13},{1... | collective-permute-start | bytes 3145736 | tf_op jit(solution)/shard_map/ppermute | solution.py:534
  8.5 3.1 %collective-permute-start = (bf16[32,128,128]{2,1,0:T(8,128)(2,1)S(1)}, bf16[32,128,128]{2,1,0:T(8,128)(2,1)S(1)}, u32[]{:S(2)}, u32[]{:S(2)}) collective-permute-start(bf16[32,128,128]{2,1,0:T(8,128)(2,1)S(1)} %get-tuple-element.38), channel_id=1, source_target_pairs={{0,12},{1,13},{2,14},{3,15},{4,0},{5,1},{6,2},{7,3},{8,4},{9,5},{1... | collective-permute-start | bytes 3145736 | tf_op jit(solution)/shard_map/ppermute | solution.py:534
  11.7 5.0 %near_sums.1 = (bf16[32,128,128]{2,1,0:T(8,128)(2,1)S(1)}, bf16[32,128,128]{2,1,0:T(8,128)(2,1)S(1)}, bf16[32,128,128]{2,1,0:T(8,128)(2,1)S(1)}, bf16[32,128,128...) custom-call(s32[128]{0:T(128)S(1)} %get-tuple-element.33.index_ref, bf16[4,128,128]{2,1,0:T(8,128)(2,1)S(1)} %get-tuple-element.34.table, ...), custom_call_target="tpu_custom_call" | custom-call | flops 805306368 | bytes 14680064 | tf_op jit(solution)/shard_map/near_sums/pallas_call | solution.py:193
  16.7 0.1 collective-permute-start.3
  16.8 2.7 %collective-permute-start.4 = (bf16[32,128,128]{2,1,0:T(8,128)(2,1)S(1)}, bf16[32,128,128]{2,1,0:T(8,128)(2,1)S(1)}, u32[]{:S(2)}, u32[]{:S(2)}) collective-permute-start(bf16[32,128,128]{2,1,0:T(8,128)(2,1)S(1)} %get-tuple-element.44), channel_id=1, source_target_pairs={{0,12},{1,13},{2,14},{3,15},{4,0},{5,1},{6,2},{7,3},{8,4},{9,5},{1... | collective-permute-start | bytes 3145736 | tf_op jit(solution)/shard_map/ppermute | solution.py:534
  19.4 4.7 %collective-permute-done.1 = bf16[32,128,128]{2,1,0:T(8,128)(2,1)S(1)} collective-permute-done((bf16[32,128,128]{2,1,0:T(8,128)(2,1)S(1)}, bf16[32,128,128]{2,1,0:T(8,128)(2,1)S(1)}, u32[]{:S(2)}, u32[]{:S(2)}) %collective-permute-start.1) | collective-permute-done | bytes 1048608 | tf_op jit(solution)/shard_map/ppermute | solution.py:534
  24.1 0.4 add_convert_fusion.refs_1_
  24.5 0.0 copy-start.3
  24.5 0.0 copy-start.4
  24.5 0.0 copy-start
  24.5 0.0 copy-start.1
  24.5 0.0 copy-start.2
  24.5 0.1 collective-permute-start.5
  24.6 0.0 collective-permute-done
  24.6 0.5 add_convert_fusion.1.refs_0_
  25.1 2.7 %collective-permute-start.2 = (bf16[32,128,128]{2,1,0:T(8,128)(2,1)S(1)}, bf16[32,128,128]{2,1,0:T(8,128)(2,1)S(1)}, u32[]{:S(2)}, u32[]{:S(2)}) collective-permute-start(bf16[32,128,128]{2,1,0:T(8,128)(2,1)S(1)} %add_convert_fusion.1.refs_0_), channel_id=1, source_target_pairs={{0,12},{1,13},{2,14},{3,15},{4,0},{5,1},{6,2},{7,3},{8,4},{9,5},{1... | collective-permute-start | bytes 3145736 | tf_op jit(solution)/shard_map/ppermute | solution.py:534
  27.9 7.4 %local_and_offset.1 = (f32[16,128,128]{2,1,0:T(8,128)S(1)}, bf16[8,128,128]{2,1,0:T(8,128)(2,1)S(1)}, bf16[8,128,128]{2,1,0:T(8,128)(2,1)S(1)}) custom-call(s32[128]{0:T(128)S(1)} %shift-left_or_fusion.index_ref, bf16[4,128,128]{2,1,0:T(8,128)(2,1)} %table_ref.3, bf16[16,128,128]{2,1,0:T(8,128)(2,1)S(1)} %copy-done.2, bf16[128,128,128]{2,1,0:T(8,128)(2,1)} %left_ref.3, ...), custom_call_target="tpu_custom_call" | custom-call | flops 1073741824 | bytes 12582912 | tf_op jit(solution)/shard_map/local_and_offset/pallas_call | solution.py:252
  35.3 0.5 collective-permute-start.6
  35.7 0.0 collective-permute-done.3.refs_1_
  35.7 0.0 collective-permute-done.4.refs_2_
  35.7 1.2 %collective-permute-done.6.refs_5_.got_offset_ref = bf16[8,128,128]{2,1,0:T(8,128)(2,1)S(1)} collective-permute-done((bf16[8,128,128]{2,1,0:T(8,128)(2,1)S(1)}, bf16[8,128,128]{2,1,0:T(8,128)(2,1)S(1)}, u32[]{:S(2)}, u32[]{:S(2)}) %collective-permute-start.6) | collective-permute-done | bytes 262176 | tf_op jit(solution)/shard_map/ppermute | solution.py:542
  36.9 9.4 %collective-permute-done.5.refs_3_ = bf16[32,128,128]{2,1,0:T(8,128)(2,1)S(1)} collective-permute-done((bf16[32,128,128]{2,1,0:T(8,128)(2,1)S(1)}, bf16[32,128,128]{2,1,0:T(8,128)(2,1)S(1)}, u32[]{:S(2)}, u32[]{:S(2)}) %collective-permute-start.5) | collective-permute-done | bytes 1048608 | tf_op jit(solution)/shard_map/ppermute | solution.py:534
  46.3 0.7 first_totals.1
  47.0 1.3 %collective-permute-start.7 = (bf16[16,128,128]{2,1,0:T(8,128)(2,1)S(1)}, bf16[16,128,128]{2,1,0:T(8,128)(2,1)S(1)}, u32[]{:S(2)}, u32[]{:S(2)}) collective-permute-start(bf16[16,128,128]{2,1,0:T(8,128)(2,1)S(1)} %get-tuple-element.47), channel_id=1, source_target_pairs={{0,1},{1,2},{2,3},{3,0},{4,5},{5,6},{6,7},{7,4},{8,9},{9,10},{10,1... | collective-permute-start | bytes 1572872 | tf_op jit(solution)/shard_map/ppermute | solution.py:534
  48.3 1.3 %collective-permute-start.8 = (bf16[16,128,128]{2,1,0:T(8,128)(2,1)S(1)}, bf16[16,128,128]{2,1,0:T(8,128)(2,1)S(1)}, u32[]{:S(2)}, u32[]{:S(2)}) collective-permute-start(bf16[16,128,128]{2,1,0:T(8,128)(2,1)S(1)} %get-tuple-element.48), channel_id=1, source_target_pairs={{0,2},{1,3},{2,0},{3,1},{4,6},{5,7},{6,4},{7,5},{8,10},{9,11},{10,... | collective-permute-start | bytes 1572872 | tf_op jit(solution)/shard_map/ppermute | solution.py:534
  49.6 1.3 %collective-permute-start.9 = (bf16[16,128,128]{2,1,0:T(8,128)(2,1)S(1)}, bf16[16,128,128]{2,1,0:T(8,128)(2,1)S(1)}, u32[]{:S(2)}, u32[]{:S(2)}) collective-permute-start(bf16[16,128,128]{2,1,0:T(8,128)(2,1)S(1)} %get-tuple-element.49), channel_id=1, source_target_pairs={{0,3},{1,0},{2,1},{3,2},{4,7},{5,4},{6,5},{7,6},{8,11},{9,8},{10,9... | collective-permute-start | bytes 1572872 | tf_op jit(solution)/shard_map/ppermute | solution.py:534
  51.0 11.3 %collective-permute-done.7.refs_1_ = bf16[16,128,128]{2,1,0:T(8,128)(2,1)S(1)} collective-permute-done((bf16[16,128,128]{2,1,0:T(8,128)(2,1)S(1)}, bf16[16,128,128]{2,1,0:T(8,128)(2,1)S(1)}, u32[]{:S(2)}, u32[]{:S(2)}) %collective-permute-start.7) | collective-permute-done | bytes 524320 | tf_op jit(solution)/shard_map/ppermute | solution.py:534
  62.3 0.6 collective-permute-done.9.refs_3_
  62.9 1.6 %coupling_and_step.1 = (f32[16,128,128]{2,1,0:T(8,128)}, bf16[8,128,128]{2,1,0:T(8,128)(2,1)S(1)}, bf16[8,128,128]{2,1,0:T(8,128)(2,1)S(1)}) custom-call(f32[16,128,128]{2,1,0:T(8,128)S(1)} %get-tuple-element.41.refs_4_.base_ref, f32[16,128,128]{2,1,0:T(8,128)S(1)} %copy-done, bf16[16,128,128]{2,1,0:T(8,128)(2,1)S(1)} %get-tuple-element.46.refs_0_, ...), custom_call_target="tpu_custom_call" | custom-call | flops 201326592 | bytes 5767168 | tf_op jit(solution)/shard_map/coupling_and_step/pallas_call | solution.py:334
  64.5 3.1 %collective-permute-start.10 = (bf16[8,128,128]{2,1,0:T(8,128)(2,1)S(1)}, bf16[8,128,128]{2,1,0:T(8,128)(2,1)S(1)}, u32[]{:S(2)}, u32[]{:S(2)}) collective-permute-start(bf16[8,128,128]{2,1,0:T(8,128)(2,1)S(1)} %get-tuple-element.53), channel_id=1, source_target_pairs={{0,16},{16,0},{32,48},{48,32},{64,80},{80,64},{96,112},{112,96},{1... | collective-permute-start | bytes 786440 | tf_op jit(solution)/shard_map/ppermute | solution.py:542
  67.6 1.2 %collective-permute-done.10.got_ref = bf16[8,128,128]{2,1,0:T(8,128)(2,1)S(1)} collective-permute-done((bf16[8,128,128]{2,1,0:T(8,128)(2,1)S(1)}, bf16[8,128,128]{2,1,0:T(8,128)(2,1)S(1)}, u32[]{:S(2)}, u32[]{:S(2)}) %collective-permute-start.10) | collective-permute-done | bytes 262176 | tf_op jit(solution)/shard_map/ppermute | solution.py:542
  68.8 0.4 compose.1
  69.2 2.7 %collective-permute-start.11 = (bf16[4,128,128]{2,1,0:T(8,128)(2,1)S(1)}, bf16[4,128,128]{2,1,0:T(8,128)(2,1)S(1)}, u32[]{:S(2)}, u32[]{:S(2)}) collective-permute-start(bf16[4,128,128]{2,1,0:T(8,128)(2,1)S(1)} %get-tuple-element.55), channel_id=1, source_target_pairs={{0,64},{16,80},{32,96},{48,112},{64,0},{80,16},{96,32},{112,48},{1... | collective-permute-start | bytes 393224 | tf_op jit(solution)/shard_map/ppermute | solution.py:538
  71.9 0.7 collective-permute-start.12
  72.6 2.0 %collective-permute-start.13 = (bf16[4,128,128]{2,1,0:T(8,128)(2,1)S(1)}, bf16[4,128,128]{2,1,0:T(8,128)(2,1)S(1)}, u32[]{:S(2)}, u32[]{:S(2)}) collective-permute-start(bf16[4,128,128]{2,1,0:T(8,128)(2,1)S(1)} %get-tuple-element.57), channel_id=1, source_target_pairs={{0,96},{16,112},{32,0},{48,16},{64,32},{80,48},{96,64},{112,80},{1... | collective-permute-start | bytes 393224 | tf_op jit(solution)/shard_map/ppermute | solution.py:538
  74.6 0.7 collective-permute-done.11.refs_1_
  75.2 3.4 %collective-permute-done.12.refs_2_ = bf16[4,128,128]{2,1,0:T(8,128)(2,1)S(1)} collective-permute-done((bf16[4,128,128]{2,1,0:T(8,128)(2,1)S(1)}, bf16[4,128,128]{2,1,0:T(8,128)(2,1)S(1)}, u32[]{:S(2)}, u32[]{:S(2)}) %collective-permute-start.12) | collective-permute-done | bytes 131104 | tf_op jit(solution)/shard_map/ppermute | solution.py:538
  78.7 0.4 run_chains.1
  79.1 2.0 %collective-permute-start.14 = (bf16[2,128,128]{2,1,0:T(8,128)(2,1)S(1)}, bf16[2,128,128]{2,1,0:T(8,128)(2,1)S(1)}, u32[]{:S(2)}, u32[]{:S(2)}) collective-permute-start(bf16[2,128,128]{2,1,0:T(8,128)(2,1)S(1)} %get-tuple-element.59), channel_id=1, source_target_pairs={{0,64},{16,80},{32,96},{48,112},{64,0},{80,16},{96,32},{112,48},{1... | collective-permute-start | bytes 196616 | tf_op jit(solution)/shard_map/ppermute | solution.py:538
  81.1 1.2 %collective-permute-start.15 = (bf16[2,128,128]{2,1,0:T(8,128)(2,1)S(1)}, bf16[2,128,128]{2,1,0:T(8,128)(2,1)S(1)}, u32[]{:S(2)}, u32[]{:S(2)}) collective-permute-start(bf16[2,128,128]{2,1,0:T(8,128)(2,1)S(1)} %get-tuple-element.60), channel_id=1, source_target_pairs={{0,32},{16,48},{32,64},{48,80},{64,96},{80,112},{96,0},{112,16},{1... | collective-permute-start | bytes 196616 | tf_op jit(solution)/shard_map/ppermute | solution.py:538
  82.3 1.5 %collective-permute-start.16 = (bf16[2,128,128]{2,1,0:T(8,128)(2,1)S(1)}, bf16[2,128,128]{2,1,0:T(8,128)(2,1)S(1)}, u32[]{:S(2)}, u32[]{:S(2)}) collective-permute-start(bf16[2,128,128]{2,1,0:T(8,128)(2,1)S(1)} %get-tuple-element.61), channel_id=1, source_target_pairs={{0,96},{16,112},{32,0},{48,16},{64,32},{80,48},{96,64},{112,80},{1... | collective-permute-start | bytes 196616 | tf_op jit(solution)/shard_map/ppermute | solution.py:538
  83.8 2.5 %collective-permute-done.15.refs_2_ = bf16[2,128,128]{2,1,0:T(8,128)(2,1)S(1)} collective-permute-done((bf16[2,128,128]{2,1,0:T(8,128)(2,1)S(1)}, bf16[2,128,128]{2,1,0:T(8,128)(2,1)S(1)}, u32[]{:S(2)}, u32[]{:S(2)}) %collective-permute-start.15) | collective-permute-done | bytes 65568 | tf_op jit(solution)/shard_map/ppermute | solution.py:538
  86.3 0.5 expand.1
  86.9 2.2 %collective-permute-start.17 = (bf16[8,128,128]{2,1,0:T(8,128)(2,1)S(1)}, bf16[8,128,128]{2,1,0:T(8,128)(2,1)S(1)}, u32[]{:S(2)}, u32[]{:S(2)}) collective-permute-start(bf16[8,128,128]{2,1,0:T(8,128)(2,1)S(1)} %get-tuple-element.62), channel_id=1, source_target_pairs={{0,16},{16,0},{32,48},{48,32},{64,80},{80,64},{96,112},{112,96},{1... | collective-permute-start | bytes 786440 | tf_op jit(solution)/shard_map/ppermute | solution.py:542
  89.0 0.8 store_rows.1.part_ref
  89.8 0.4 collective-permute-done.17.got_ref
  90.2 0.8 add_rows.1
  (11 shorter events, 0.0 us)
Async XLA Ops:
  6.5 17.6 %collective-permute-start.1 = (bf16[32,128,128]{2,1,0:T(8,128)(2,1)S(1)}, bf16[32,128,128]{2,1,0:T(8,128)(2,1)S(1)}, u32[]{:S(2)}, u32[]{:S(2)}) collective-permute-start(bf16[32,128,128]{2,1,0:T(8,128)(2,1)S(1)} %get-tuple-element.40), channel_id=1, source_target_pairs={{0,4},{1,5},{2,6},{3,7},{4,8},{5,9},{6,10},{7,11},{8,12},{9,13},{1... | collective-permute-start | bytes 3145736 | tf_op jit(solution)/shard_map/ppermute | solution.py:534
  8.5 16.1 %collective-permute-start = (bf16[32,128,128]{2,1,0:T(8,128)(2,1)S(1)}, bf16[32,128,128]{2,1,0:T(8,128)(2,1)S(1)}, u32[]{:S(2)}, u32[]{:S(2)}) collective-permute-start(bf16[32,128,128]{2,1,0:T(8,128)(2,1)S(1)} %get-tuple-element.38), channel_id=1, source_target_pairs={{0,12},{1,13},{2,14},{3,15},{4,0},{5,1},{6,2},{7,3},{8,4},{9,5},{1... | collective-permute-start | bytes 3145736 | tf_op jit(solution)/shard_map/ppermute | solution.py:534
  16.7 19.1 %collective-permute-start.3 = (bf16[32,128,128]{2,1,0:T(8,128)(2,1)S(1)}, bf16[32,128,128]{2,1,0:T(8,128)(2,1)S(1)}, u32[]{:S(2)}, u32[]{:S(2)}) collective-permute-start(bf16[32,128,128]{2,1,0:T(8,128)(2,1)S(1)} %get-tuple-element.43), channel_id=1, source_target_pairs={{0,4},{1,5},{2,6},{3,7},{4,8},{5,9},{6,10},{7,11},{8,12},{9,13},{1... | collective-permute-start | bytes 3145736 | tf_op jit(solution)/shard_map/ppermute | solution.py:534
  16.8 19.0 %collective-permute-start.4 = (bf16[32,128,128]{2,1,0:T(8,128)(2,1)S(1)}, bf16[32,128,128]{2,1,0:T(8,128)(2,1)S(1)}, u32[]{:S(2)}, u32[]{:S(2)}) collective-permute-start(bf16[32,128,128]{2,1,0:T(8,128)(2,1)S(1)} %get-tuple-element.44), channel_id=1, source_target_pairs={{0,12},{1,13},{2,14},{3,15},{4,0},{5,1},{6,2},{7,3},{8,4},{9,5},{1... | collective-permute-start | bytes 3145736 | tf_op jit(solution)/shard_map/ppermute | solution.py:534
  24.5 3.3 %copy-start.3 = (s32[128]{0:T(128)S(1)}, s32[128]{0:T(128)}, u32[]{:S(2)}) copy-start(s32[128]{0:T(128)} %param.26) | copy-start | bytes 1540
  24.5 3.3 %copy-start.4 = (s32[128]{0:T(128)S(1)}, s32[128]{0:T(128)}, u32[]{:S(2)}) copy-start(s32[128]{0:T(128)} %param.25) | copy-start | bytes 1540
  24.5 3.3 %copy-start = (f32[16,128,128]{2,1,0:T(8,128)S(1)}, f32[16,128,128]{2,1,0:T(8,128)}, u32[]{:S(2)}) copy-start(f32[16,128,128]{2,1,0:T(8,128)} %diag_ref.3) | copy-start | bytes 3145732
  24.5 3.3 %copy-start.1 = (f32[16,128,128]{2,1,0:T(8,128)S(1)}, f32[16,128,128]{2,1,0:T(8,128)}, u32[]{:S(2)}) copy-start(f32[16,128,128]{2,1,0:T(8,128)} %seed_ref.1) | copy-start | bytes 3145732
  24.5 3.3 %copy-start.2 = (bf16[16,128,128]{2,1,0:T(8,128)(2,1)S(1)}, bf16[16,128,128]{2,1,0:T(8,128)(2,1)}, u32[]{:S(2)}) copy-start(bf16[16,128,128]{2,1,0:T(8,128)(2,1)} %coupling_ref.1) | copy-start | bytes 1572868
  24.5 21.7 %collective-permute-start.5 = (bf16[32,128,128]{2,1,0:T(8,128)(2,1)S(1)}, bf16[32,128,128]{2,1,0:T(8,128)(2,1)S(1)}, u32[]{:S(2)}, u32[]{:S(2)}) collective-permute-start(bf16[32,128,128]{2,1,0:T(8,128)(2,1)S(1)} %add_convert_fusion.refs_1_), channel_id=1, source_target_pairs={{0,4},{1,5},{2,6},{3,7},{4,8},{5,9},{6,10},{7,11},{8,12},{9,13},{1... | collective-permute-start | bytes 3145736 | tf_op jit(solution)/shard_map/ppermute | solution.py:534
  25.1 21.2 %collective-permute-start.2 = (bf16[32,128,128]{2,1,0:T(8,128)(2,1)S(1)}, bf16[32,128,128]{2,1,0:T(8,128)(2,1)S(1)}, u32[]{:S(2)}, u32[]{:S(2)}) collective-permute-start(bf16[32,128,128]{2,1,0:T(8,128)(2,1)S(1)} %add_convert_fusion.1.refs_0_), channel_id=1, source_target_pairs={{0,12},{1,13},{2,14},{3,15},{4,0},{5,1},{6,2},{7,3},{8,4},{9,5},{1... | collective-permute-start | bytes 3145736 | tf_op jit(solution)/shard_map/ppermute | solution.py:534
  35.3 1.6 %collective-permute-start.6 = (bf16[8,128,128]{2,1,0:T(8,128)(2,1)S(1)}, bf16[8,128,128]{2,1,0:T(8,128)(2,1)S(1)}, u32[]{:S(2)}, u32[]{:S(2)}) collective-permute-start(bf16[8,128,128]{2,1,0:T(8,128)(2,1)S(1)} %get-tuple-element.45), channel_id=1, source_target_pairs={{0,16},{16,0},{32,48},{48,32},{64,80},{80,64},{96,112},{112,96},{1... | collective-permute-start | bytes 786440 | tf_op jit(solution)/shard_map/ppermute | solution.py:542
  47.0 15.2 %collective-permute-start.7 = (bf16[16,128,128]{2,1,0:T(8,128)(2,1)S(1)}, bf16[16,128,128]{2,1,0:T(8,128)(2,1)S(1)}, u32[]{:S(2)}, u32[]{:S(2)}) collective-permute-start(bf16[16,128,128]{2,1,0:T(8,128)(2,1)S(1)} %get-tuple-element.47), channel_id=1, source_target_pairs={{0,1},{1,2},{2,3},{3,0},{4,5},{5,6},{6,7},{7,4},{8,9},{9,10},{10,1... | collective-permute-start | bytes 1572872 | tf_op jit(solution)/shard_map/ppermute | solution.py:534
  48.3 13.9 %collective-permute-start.8 = (bf16[16,128,128]{2,1,0:T(8,128)(2,1)S(1)}, bf16[16,128,128]{2,1,0:T(8,128)(2,1)S(1)}, u32[]{:S(2)}, u32[]{:S(2)}) collective-permute-start(bf16[16,128,128]{2,1,0:T(8,128)(2,1)S(1)} %get-tuple-element.48), channel_id=1, source_target_pairs={{0,2},{1,3},{2,0},{3,1},{4,6},{5,7},{6,4},{7,5},{8,10},{9,11},{10,... | collective-permute-start | bytes 1572872 | tf_op jit(solution)/shard_map/ppermute | solution.py:534
  49.6 13.2 %collective-permute-start.9 = (bf16[16,128,128]{2,1,0:T(8,128)(2,1)S(1)}, bf16[16,128,128]{2,1,0:T(8,128)(2,1)S(1)}, u32[]{:S(2)}, u32[]{:S(2)}) collective-permute-start(bf16[16,128,128]{2,1,0:T(8,128)(2,1)S(1)} %get-tuple-element.49), channel_id=1, source_target_pairs={{0,3},{1,0},{2,1},{3,2},{4,7},{5,4},{6,5},{7,6},{8,11},{9,8},{10,9... | collective-permute-start | bytes 1572872 | tf_op jit(solution)/shard_map/ppermute | solution.py:534
  64.5 4.3 %collective-permute-start.10 = (bf16[8,128,128]{2,1,0:T(8,128)(2,1)S(1)}, bf16[8,128,128]{2,1,0:T(8,128)(2,1)S(1)}, u32[]{:S(2)}, u32[]{:S(2)}) collective-permute-start(bf16[8,128,128]{2,1,0:T(8,128)(2,1)S(1)} %get-tuple-element.53), channel_id=1, source_target_pairs={{0,16},{16,0},{32,48},{48,32},{64,80},{80,64},{96,112},{112,96},{1... | collective-permute-start | bytes 786440 | tf_op jit(solution)/shard_map/ppermute | solution.py:542
  69.2 6.1 %collective-permute-start.11 = (bf16[4,128,128]{2,1,0:T(8,128)(2,1)S(1)}, bf16[4,128,128]{2,1,0:T(8,128)(2,1)S(1)}, u32[]{:S(2)}, u32[]{:S(2)}) collective-permute-start(bf16[4,128,128]{2,1,0:T(8,128)(2,1)S(1)} %get-tuple-element.55), channel_id=1, source_target_pairs={{0,64},{16,80},{32,96},{48,112},{64,0},{80,16},{96,32},{112,48},{1... | collective-permute-start | bytes 393224 | tf_op jit(solution)/shard_map/ppermute | solution.py:538
  71.9 6.8 %collective-permute-start.12 = (bf16[4,128,128]{2,1,0:T(8,128)(2,1)S(1)}, bf16[4,128,128]{2,1,0:T(8,128)(2,1)S(1)}, u32[]{:S(2)}, u32[]{:S(2)}) collective-permute-start(bf16[4,128,128]{2,1,0:T(8,128)(2,1)S(1)} %get-tuple-element.56), channel_id=1, source_target_pairs={{0,32},{16,48},{32,64},{48,80},{64,96},{80,112},{96,0},{112,16},{1... | collective-permute-start | bytes 393224 | tf_op jit(solution)/shard_map/ppermute | solution.py:538
  72.6 6.1 %collective-permute-start.13 = (bf16[4,128,128]{2,1,0:T(8,128)(2,1)S(1)}, bf16[4,128,128]{2,1,0:T(8,128)(2,1)S(1)}, u32[]{:S(2)}, u32[]{:S(2)}) collective-permute-start(bf16[4,128,128]{2,1,0:T(8,128)(2,1)S(1)} %get-tuple-element.57), channel_id=1, source_target_pairs={{0,96},{16,112},{32,0},{48,16},{64,32},{80,48},{96,64},{112,80},{1... | collective-permute-start | bytes 393224 | tf_op jit(solution)/shard_map/ppermute | solution.py:538
  79.1 4.7 %collective-permute-start.14 = (bf16[2,128,128]{2,1,0:T(8,128)(2,1)S(1)}, bf16[2,128,128]{2,1,0:T(8,128)(2,1)S(1)}, u32[]{:S(2)}, u32[]{:S(2)}) collective-permute-start(bf16[2,128,128]{2,1,0:T(8,128)(2,1)S(1)} %get-tuple-element.59), channel_id=1, source_target_pairs={{0,64},{16,80},{32,96},{48,112},{64,0},{80,16},{96,32},{112,48},{1... | collective-permute-start | bytes 196616 | tf_op jit(solution)/shard_map/ppermute | solution.py:538
  81.1 5.2 %collective-permute-start.15 = (bf16[2,128,128]{2,1,0:T(8,128)(2,1)S(1)}, bf16[2,128,128]{2,1,0:T(8,128)(2,1)S(1)}, u32[]{:S(2)}, u32[]{:S(2)}) collective-permute-start(bf16[2,128,128]{2,1,0:T(8,128)(2,1)S(1)} %get-tuple-element.60), channel_id=1, source_target_pairs={{0,32},{16,48},{32,64},{48,80},{64,96},{80,112},{96,0},{112,16},{1... | collective-permute-start | bytes 196616 | tf_op jit(solution)/shard_map/ppermute | solution.py:538
  82.3 4.0 %collective-permute-start.16 = (bf16[2,128,128]{2,1,0:T(8,128)(2,1)S(1)}, bf16[2,128,128]{2,1,0:T(8,128)(2,1)S(1)}, u32[]{:S(2)}, u32[]{:S(2)}) collective-permute-start(bf16[2,128,128]{2,1,0:T(8,128)(2,1)S(1)} %get-tuple-element.61), channel_id=1, source_target_pairs={{0,96},{16,112},{32,0},{48,16},{64,32},{80,48},{96,64},{112,80},{1... | collective-permute-start | bytes 196616 | tf_op jit(solution)/shard_map/ppermute | solution.py:538
  86.9 3.3 %collective-permute-start.17 = (bf16[8,128,128]{2,1,0:T(8,128)(2,1)S(1)}, bf16[8,128,128]{2,1,0:T(8,128)(2,1)S(1)}, u32[]{:S(2)}, u32[]{:S(2)}) collective-permute-start(bf16[8,128,128]{2,1,0:T(8,128)(2,1)S(1)} %get-tuple-element.62), channel_id=1, source_target_pairs={{0,16},{16,0},{32,48},{48,32},{64,80},{80,64},{96,112},{112,96},{1... | collective-permute-start | bytes 786440 | tf_op jit(solution)/shard_map/ppermute | solution.py:542
